TPU v7x, 32 devices: a whole 2x2x4 slice. The times are simulated.
32 devices in a mesh: section: 8 (over z, x), dp: 4 (over y, core).
Axes of the slice: x: 2, y: 2, z: 4, core: 2. Of those that a mesh axis runs over, the one named last changes fastest.
Arguments:
- act_in: bfloat16 [8, 128, 2048], P('section', None, 'dp'), may hold values from -6 to 6
- saved_act: bfloat16 [8, 128, 2048], P('section', None, 'dp'), may hold values from -6 to 6
- cotangent: bfloat16 [8, 128, 2048], P('section', None, 'dp'), may hold values from -6 to 6
- weight_xz: bfloat16 [8, 2048, 8192], P('section', 'dp'), may hold values from -0.125 to 0.125
- weight_bcdt: bfloat16 [8, 320, 2048], P('section', None, 'dp'), may hold values from -0.125 to 0.125
- weight_out: bfloat16 [8, 4096, 2048], P('section', None, 'dp'), may hold values from -0.09375 to 0.09375
- conv_x: float32 [8, 4, 4096], P('section', None, 'dp'), may hold values from -3 to 3
- conv_bc: float32 [8, 4, 256], P('section'), may hold values from -3 to 3
- dt_bias: float32 [8, 64], P('section', 'dp'), may hold values from -8 to -2
- a_log: float32 [8, 64], P('section', 'dp'), may hold values from 0 to 2.7
- d_skip: float32 [8, 64], P('section', 'dp'), may hold values from 0.5 to 1.5
- norm_gain: float32 [8, 4096], P('section', 'dp'), may hold values from 0.1 to 1.9
Outputs:
- next_act: bfloat16 [8, 128, 2048], P('section', None, 'dp')
- prev_grad: bfloat16 [8, 128, 2048], P('section', None, 'dp')
- grad_xz: float32 [8, 2048, 8192], P('section', 'dp')
- grad_bcdt: float32 [8, 320, 2048], P('section', None, 'dp')
- grad_out: float32 [8, 4096, 2048], P('section', None, 'dp')
All inputs are finite; a program needn't handle non-finite values.
Results may differ from a plain program's by a relative error of at most 0.0084.
Values may be sent and summed in bfloat16 or wider, within the bound.
A program may use at most 128 MiB of HBM per device.

v0:
```python
import jax
import jax.numpy as jnp
from jax import lax
from jax.sharding import PartitionSpec as P

D = 2048
HEAD_DIM = 64
NSTATE = 128
HEADS = 64
SEQ = 128
INNER = 4096


def from_behind(x, axis, by):
    length = lax.axis_size(axis)
    return lax.ppermute(x, axis, [(i, (i + by) % length) for i in range(length)])


def causal_conv(values, kernel_taps):
    kernel = kernel_taps.shape[0]
    length = values.shape[1]
    padded = jnp.pad(values, ((0, 0), (kernel - 1, 0), (0, 0)))
    running = jnp.zeros_like(values)
    for offset in range(kernel):
        running = running + kernel_taps[offset] * padded[:, offset : offset + length]
    return running


def map_scores(maps):
    input_map = maps[:, :, :NSTATE]
    output_map = maps[:, :, NSTATE:]
    return lax.dot_general(
        output_map, input_map, (((2,), (2,)), ((0,), (0,))), preferred_element_type=jnp.float32
    )


def map_grads(d_scores, maps):
    values = maps.astype(jnp.float32)
    input_map = values[:, :, :NSTATE]
    output_map = values[:, :, NSTATE:]
    d_input = jnp.einsum("bts,btn->bsn", d_scores, output_map, precision=lax.Precision.HIGHEST)
    d_output = jnp.einsum("bts,bsn->btn", d_scores, input_map, precision=lax.Precision.HIGHEST)
    return jnp.concatenate([d_input, d_output], axis=2)


def mixer(proj_x, proj_z, proj_dt, scores, conv_taps, dt_offset, log_rate, skip_gain):
    batch, length, width = proj_x.shape
    nheads = dt_offset.shape[0]
    head_width = width // nheads
    xconv = jax.nn.silu(causal_conv(proj_x, conv_taps))
    steps = jax.nn.softplus(proj_dt + dt_offset)
    cumul = jnp.cumsum(steps * -jnp.exp(log_rate), axis=1)
    position = jnp.arange(length)
    causal = (position[:, None] >= position[None, :])[None, None]
    heads_cum = jnp.swapaxes(cumul, 1, 2)
    spread = heads_cum[:, :, :, None] - heads_cum[:, :, None, :]
    decay = jnp.where(causal, jnp.exp(jnp.where(causal, spread, 0.0)), 0.0)
    weights = decay * scores[:, None] * jnp.swapaxes(steps, 1, 2)[:, :, None, :]
    heads_in = xconv.reshape(batch, length, nheads, head_width)
    result = jnp.einsum("bhts,bshp->bthp", weights, heads_in, precision=lax.Precision.HIGHEST)
    result = result + skip_gain[None, None, :, None] * heads_in
    gate_in = jax.nn.silu(proj_z.reshape(batch, length, nheads, head_width))
    return (result * gate_in).reshape(batch * length, width)


def times_transposed(left, right):
    return lax.dot_general(
        left, right, (((1,), (1,)), ((), ())), preferred_element_type=jnp.float32
    )


def transposed_times(left, right):
    return lax.dot_general(
        left, right, (((0,), (0,)), ((), ())), preferred_element_type=jnp.float32
    )


def feature_sum(values):
    return lax.psum(jnp.sum(values, axis=1), "dp")


def gate_sum(values):
    return lax.psum(jnp.sum(values, axis=1), "dp")


def send_along(row_block, direction):
    return from_behind(row_block, "section", direction)


def per_device(
    act_in,
    saved_act,
    cotangent,
    weight_xz,
    weight_bcdt,
    weight_out,
    conv_x,
    conv_bc,
    dt_bias,
    a_log,
    d_skip,
    norm_gain,
):
    input_rows = act_in[0]
    saved_rows = saved_act[0]
    cot_rows = cotangent[0]
    local_xz = weight_xz[0]
    local_bcdt = weight_bcdt[0]
    local_out = weight_out[0]
    taps_x = conv_x[0]
    taps_bc = conv_bc[0]
    dt_offset = dt_bias[0]
    log_rate = a_log[0]
    skip_gain = d_skip[0]
    gain_local = norm_gain[0]
    own_heads = dt_offset.shape[0]
    head_first = lax.axis_index("dp") * own_heads
    map_cols = 2 * NSTATE

    def whole_act(pre_part):
        batches = pre_part.shape[0] // SEQ
        conv_in = pre_part.reshape(batches, SEQ, map_cols)
        return jax.nn.silu(causal_conv(conv_in, taps_bc)).reshape(pre_part.shape)

    def project(rows):
        values = rows.astype(jnp.float32)
        scales = lax.rsqrt(feature_sum(values * values)[:, None] / D + 1e-05)
        normed = (values * scales).astype(jnp.bfloat16)
        part_xz = jnp.dot(normed, local_xz, preferred_element_type=jnp.float32)
        part_bcdt = times_transposed(normed, local_bcdt)
        own_xz = lax.psum_scatter(part_xz, "dp", scatter_dimension=1, tiled=True)
        whole_cols = lax.psum(part_bcdt, "dp")
        pre_part = whole_cols[:, :map_cols]
        maps = whole_act(pre_part).astype(jnp.bfloat16)
        own_dt = lax.dynamic_slice_in_dim(whole_cols[:, map_cols:], head_first, own_heads, 1)
        return (values, normed, scales, own_xz, pre_part, maps, own_dt)

    def gate_parts(projected):
        own_xz = projected[3]
        maps = projected[5]
        own_dt = projected[6]
        batches = own_xz.shape[0] // SEQ
        width = own_heads * HEAD_DIM
        split_xz = own_xz.reshape(batches, SEQ, own_heads, 2, HEAD_DIM)
        mix_x = split_xz[:, :, :, 0].reshape(batches, SEQ, width)
        mix_z = split_xz[:, :, :, 1].reshape(batches, SEQ, width)
        maps_three = maps.reshape(batches, SEQ, map_cols)
        scores = map_scores(maps_three)

        def local_mix(in_x, in_z, in_dt, in_scores):
            return mixer(in_x, in_z, in_dt, in_scores, taps_x, dt_offset, log_rate, skip_gain)

        gated, mix_back = jax.vjp(
            local_mix, mix_x, mix_z, own_dt.reshape(batches, SEQ, own_heads), scores
        )
        inverse = lax.rsqrt(gate_sum(gated * gated)[:, None] / INNER + 1e-05)
        mixed_in = (gated * inverse * gain_local).astype(jnp.bfloat16)
        return (gated, mix_back, inverse, mixed_in, maps_three)

    forward_proj = project(input_rows)
    back_proj = project(saved_rows)
    forward_mixed = gate_parts(forward_proj)[3]
    mixed = jnp.dot(
        lax.all_gather(forward_mixed, "dp", axis=1, tiled=True),
        local_out,
        preferred_element_type=jnp.float32,
    )
    section_out = (input_rows.astype(jnp.float32) + mixed).astype(jnp.bfloat16)
    next_act = send_along(section_out, 1)
    values, normed, scales, own_xz, pre_part, maps, own_dt = back_proj
    gated, mix_back, inverse, mixed_in, maps_three = gate_parts(back_proj)
    row_count = values.shape[0]
    grad_out = transposed_times(lax.all_gather(mixed_in, "dp", axis=1, tiled=True), cot_rows)
    d_mixed = lax.psum_scatter(
        times_transposed(cot_rows, local_out), "dp", scatter_dimension=1, tiled=True
    )
    dots = gate_sum(d_mixed * gain_local * gated)
    d_gated = (
        inverse * gain_local * d_mixed
        - gated * (inverse * inverse * inverse) * dots[:, None] / INNER
    )
    d_px, d_pz, d_pdt, d_scores = mix_back(d_gated)
    d_maps = map_grads(d_scores, maps_three).reshape(row_count, map_cols)
    d_dt_full = lax.dynamic_update_slice_in_dim(
        jnp.zeros((row_count, HEADS), jnp.float32),
        d_pdt.reshape(row_count, own_heads),
        head_first,
        1,
    )
    map_part = jnp.concatenate([d_maps, d_dt_full], axis=1)
    summed = lax.psum(map_part, "dp")
    conv_out, conv_back = jax.vjp(whole_act, pre_part)
    d_pre = conv_back(summed[:, :map_cols])[0]
    round_bcdt = jnp.concatenate([d_pre, summed[:, map_cols:]], axis=1).astype(jnp.bfloat16)
    own_round = (
        jnp.stack(
            [
                d_px.reshape(row_count, own_heads, HEAD_DIM),
                d_pz.reshape(row_count, own_heads, HEAD_DIM),
            ],
            axis=2,
        )
        .reshape(row_count, own_heads * 2 * HEAD_DIM)
        .astype(jnp.bfloat16)
    )
    round_xz = lax.all_gather(own_round, "dp", axis=1, tiled=True)
    grad_xz = transposed_times(normed, round_xz)
    grad_bcdt = transposed_times(round_bcdt, normed)
    d_normed = times_transposed(round_xz, local_xz)
    d_normed = d_normed + jnp.dot(round_bcdt, local_bcdt, preferred_element_type=jnp.float32)
    inner_sum = feature_sum(d_normed * values)[:, None]
    d_norm_in = scales * d_normed - values * (scales * scales * scales) * inner_sum / D
    d_input = (cot_rows.astype(jnp.float32) + d_norm_in).astype(jnp.bfloat16)
    prev_grad = send_along(d_input, -1)
    return (next_act[None], prev_grad[None], grad_xz[None], grad_bcdt[None], grad_out[None])


def solution(mesh):
    return jax.shard_map(
        per_device,
        mesh=mesh,
        in_specs=(
            P("section", None, "dp"),
            P("section", None, "dp"),
            P("section", None, "dp"),
            P("section", "dp", None),
            P("section", None, "dp"),
            P("section", None, "dp"),
            P("section", None, "dp"),
            P("section", None, None),
            P("section", "dp"),
            P("section", "dp"),
            P("section", "dp"),
            P("section", "dp"),
        ),
        out_specs=(
            P("section", None, "dp"),
            P("section", None, "dp"),
            P("section", "dp", None),
            P("section", None, "dp"),
            P("section", None, "dp"),
        ),
        check_vma=False,
    )
```

profile of v0, /device:TPU:0, one launch (start us, length us, event | category | flops | bytes accessed | tf_op | source)
XLA Modules:
  0.0 311.2 jit_solution(6612498661934579519)
XLA Ops:
  8.3 8.4 %psum.66 = f32[128]{0:T(128)S(1)} all-reduce(f32[128]{0:T(128)S(1)} %fusion.86), channel_id=1, replica_groups=mesh['section'=8,'dp'=4] {'dp'}, use_global_device_ids=true, to_apply=%region_8.9 | all-reduce | flops 128 | bytes 1024 | tf_op jit(solution)/shard_map/psum | solution.py:79
  17.2 1.9 fusion.80
  19.2 6.8 %fusion.2 = f32[128,8192]{1,0:T(8,128)} fusion(bf16[1,512,8192]{2,1,0:T(8,128)(2,1)} %param.15, bf16[1,128,512]{2,1,0:T(8,128)(2,1)} %param.13, f32[128]{0:T(128)S(1)} %get-tuple-element.49), kind=kOutput, calls=%fused_computation.3 | convolution fusion | flops 1073938432 | bytes 12714496 | tf_op jit(solution)/shard_map/dot_general | solution.py:129
  26.9 5.0 %fusion.6 = f32[128,4096]{1,0:T(8,128)} fusion(bf16[1,4096,512]{2,1,0:T(8,128)(2,1)} %param.17, bf16[1,128,512]{2,1,0:T(8,128)(2,1)S(1)} %copy-done.5), kind=kOutput, calls=%fused_computation.8 | convolution fusion | flops 536870912 | bytes 6422528 | tf_op jit(solution)/shard_map/dot_general | solution.py:67
  32.2 19.0 %all-reduce.18.cloned.1.call-done = f32[128,320]{0,1:T(8,128)} async-done(((f32[128,320]{0,1:T(8,128)}), f32[128,320]{0,1:T(8,128)}) %all-reduce.18.cloned.1.call-update) | async-done | bytes 163856 | tf_op jit(solution)/shard_map/psum | solution.py:132
  53.3 1.9 multiply_convert_fusion.2
  55.4 43.6 %reduce-scatter.6.cloned.1.call-done = f32[128,2048]{1,0:T(8,128)} async-done(((f32[128,8192]{1,0:T(8,128)}), f32[128,2048]{1,0:T(8,128)}) %reduce-scatter.6.cloned.1.call-update) | async-done | bytes 1048592 | tf_op jit(solution)/shard_map/reduce_scatter | solution.py:131
  99.0 1.5 copy.55
  101.8 3.0 multiply_reduce_fusion.3
  104.8 1.2 copy.60
  106.1 27.5 %reduce-scatter.8.cloned.1.call-done = f32[128,1024]{1,0:T(8,128)} async-done(((f32[128,4096]{1,0:T(8,128)}), f32[128,1024]{1,0:T(8,128)}) %reduce-scatter.8.cloned.1.call-update) | async-done | bytes 524304 | tf_op jit(solution)/shard_map/reduce_scatter | solution.py:174
  134.7 5.8 %all-reduce.13 = (f32[128]{0:T(128)S(1)}, f32[128]{0:T(128)S(1)}, f32[128]{0:T(128)S(1)}) all-reduce(f32[128]{0:T(128)S(1)} %fusion.84, f32[128]{0:T(128)S(1)} %multiply_reduce_fusion.2, f32[128]{0:T(128)S(1)} %get-tuple-element.20), channel_id=1, replica_groups=mesh['section'=8,'dp'=4] {'dp'}, use_global_device_ids=true, to_apply=%region_1.0 | all-reduce | flops 384 | bytes 3072 | tf_op jit(solution)/shard_map/psum | solution.py:79
  140.5 6.7 %fusion.4 = f32[128,8192]{1,0:T(8,128)} fusion(bf16[1,512,8192]{2,1,0:T(8,128)(2,1)} %param.15, bf16[1,128,512]{2,1,0:T(8,128)(2,1)S(1)} %copy-done.3, f32[128]{0:T(128)S(1)} %add_rsqrt_fusion.3), kind=kOutput, calls=%fused_computation.5 | convolution fusion | flops 1073938432 | bytes 12714496 | tf_op jit(solution)/shard_map/dot_general | solution.py:129
  147.5 2.0 multiply_convert_fusion
  149.7 4.2 %fusion.32 = (f32[16,128]{1,0:T(8,128)S(1)}, f32[16,128]{1,0:T(8,128)S(1)}, f32[16,128]{1,0:T(8,128)}, f32[128,128]{1,0:T(8,128)S(1)}) fusion(f32[16,128]{1,0:T(8,128)S(1)} %get-tuple-element.37, f32[128,128]{1,0:T(8,128)S(1)} %fusion.125, f32[16,128]{1,0:T(8,128)S(1)} %copy.57, pred[128,128]{1,0:T(8,128)(4,1)S(1)} %iota_compare_fusion, ...), kind=kOutput, calls=%fused_computation.47 | convolution fusion | flops 205891584 | bytes 1769472 | tf_op jit(solution)/shard_map/transpose(jvp(bhts,bshp->bthp))/dot_general | solution.py:60
  157.2 1.7 fusion.82
  159.1 2.3 fusion.10
  161.7 31.3 %reduce-scatter.4.cloned.1.call-done = f32[128,2048]{1,0:T(8,128)} async-done(((f32[128,8192]{1,0:T(8,128)}), f32[128,2048]{1,0:T(8,128)}) %reduce-scatter.4.cloned.1.call-update) | async-done | bytes 1048592 | tf_op jit(solution)/shard_map/reduce_scatter | solution.py:131
  193.0 1.5 copy.49
  194.6 1.9 broadcast_multiply_fusion.1
  198.9 28.8 %all-reduce.20.cloned.1.call-done = (f32[128,320]{0,1:T(8,128)}, f32[128,320]{0,1:T(8,128)}) async-done(((f32[128,320]{0,1:T(8,128)}, f32[128,320]{0,1:T(8,128)}), (f32[128,320]{0,1:T(8,128)}, f32[128,320]{0,1:T(8,128)})) %all-reduce.20.cloned.1.call-update) | async-done | bytes 327696 | tf_op jit(solution)/shard_map/psum | solution.py:132
  233.2 3.3 %multiply_reduce_fusion.4 = (f32[128]{0:T(128)S(1)}, f32[1,128,16,64]{1,3,2,0:T(8,128)S(1)}) fusion(f32[1,128,16,2,64]{1,4,3,2,0:T(8,128)S(1)} %bitcast.276, f32[1,128,16,64]{1,3,2,0:T(8,128)} %bitcast.288, f32[16]{0:T(128)S(1)} %bitcast.320, f32[128,16,64]{0,2,1:T(8,128)} %bitcast.289, f32[16,128]{1,0:T(8,128)S(1)} %get-tuple-element.35, ...), kind=kOutput, calls=%fused_computation.94 | convolution fusion | flops 203816832 | bytes 2204672 | tf_op jit(solution)/shard_map/jvp(bhts,bshp->bthp)/dot_general | solution.py:60
  236.8 15.6 %all-gather.6.cloned.1.call-done = bf16[128,8192]{0,1:T(8,128)(2,1)} async-done(((bf16[128,2048]{0,1:T(8,128)(2,1)}), bf16[128,8192]{0,1:T(8,128)(2,1)}) %all-gather.6.cloned.1.call-update) | async-done | bytes 2097168 | tf_op jit(solution)/shard_map/all_gather | solution.py:206
  252.3 6.9 %fusion = f32[128,512]{1,0:T(8,128)S(1)} fusion(bf16[128,8192]{0,1:T(8,128)(2,1)} %all-gather.6.cloned.1.call-done, bf16[1,512,8192]{2,1,0:T(8,128)(2,1)} %param.15), kind=kOutput, calls=%fused_computation.1 | convolution fusion | flops 1073741824 | bytes 10747904 | tf_op jit(solution)/shard_map/dot_general | solution.py:67
  259.6 6.3 %all-reduce.12 = (f32[128]{0:T(128)S(1)}, f32[128]{0:T(128)S(1)}) all-reduce(f32[128]{0:T(128)S(1)} %get-tuple-element.53, f32[128]{0:T(128)S(1)} %get-tuple-element.55), channel_id=1, replica_groups=mesh['section'=8,'dp'=4] {'dp'}, use_global_device_ids=true, to_apply=%region_6.7 | all-reduce | flops 256 | bytes 2048 | tf_op jit(solution)/shard_map/psum | solution.py:83
  267.9 3.4 %all-gather.8.cloned.1.call-done = bf16[128,4096]{1,0:T(8,128)(2,1)} async-done(((bf16[128,1024]{1,0:T(8,128)(2,1)}), bf16[128,4096]{1,0:T(8,128)(2,1)}) %all-gather.8.cloned.1.call-update) | async-done | bytes 1048592 | tf_op jit(solution)/shard_map/all_gather | solution.py:173
  271.3 5.9 %convolution_bitcast_fusion.1 = f32[1,4096,512]{2,1,0:T(8,128)} fusion(bf16[128,4096]{1,0:T(8,128)(2,1)} %all-gather.8.cloned.1.call-done, bf16[1,128,512]{2,1,0:T(8,128)(2,1)S(1)} %copy-done.5), kind=kOutput, calls=%fused_computation.7 | convolution fusion | flops 536870912 | bytes 9568256 | tf_op jit(solution)/shard_map/dot_general | solution.py:73
  277.4 4.3 %collective-permute-start.1 = (bf16[128,512]{1,0:T(8,128)(2,1)S(1)}, bf16[128,512]{1,0:T(8,128)(2,1)S(1)}, u32[]{:S(2)}, u32[]{:S(2)}) collective-permute-start(bf16[128,512]{1,0:T(8,128)(2,1)S(1)} %fusion.91), channel_id=1, source_target_pairs={{0,28},{4,0},{8,4},{12,8},{16,12},{20,16},{24,20},{28,24},{1,29},{... | collective-permute-start | bytes 393224 | tf_op jit(solution)/shard_map/ppermute | solution.py:16
  281.7 8.0 %all-gather.4.cloned.1.call-done = bf16[128,4096]{1,0:T(8,128)(2,1)} async-done(((bf16[128,1024]{1,0:T(8,128)(2,1)}), bf16[128,4096]{1,0:T(8,128)(2,1)}) %all-gather.4.cloned.1.call-update) | async-done | bytes 1048592 | tf_op jit(solution)/shard_map/all_gather | solution.py:164
  289.7 3.2 %fusion.17 = bf16[128,512]{1,0:T(8,128)(2,1)S(1)} fusion(bf16[128,4096]{1,0:T(8,128)(2,1)} %all-gather.4.cloned.1.call-done, bf16[1,4096,512]{2,1,0:T(8,128)(2,1)} %param.17, bf16[1,128,512]{2,1,0:T(8,128)(2,1)S(1)} %copy-done.4), kind=kOutput, calls=%fused_computation.28 | convolution fusion | flops 537067520 | bytes 5505024 | tf_op jit(solution)/shard_map/dot_general | solution.py:163
  292.9 1.5 collective-permute-start
  294.4 8.6 %convolution_bitcast_fusion = f32[1,512,8192]{2,1,0:T(8,128)} fusion(bf16[128,8192]{0,1:T(8,128)(2,1)S(1)} %copy-done.1, bf16[1,128,512]{2,1,0:T(8,128)(2,1)S(1)} %copy-done.2, f32[128]{0:T(128)S(1)} %get-tuple-element.49), kind=kOutput, calls=%fused_computation | convolution fusion | flops 1073938432 | bytes 19005952 | tf_op jit(solution)/shard_map/dot_general | solution.py:73
  (131 shorter events, 23.6 us)
Async XLA Ops:
  7.2 10.1 %copy-start = (bf16[1,320,512]{2,1,0:T(8,128)(2,1)S(1)}, bf16[1,320,512]{2,1,0:T(8,128)(2,1)}, u32[]{:S(2)}) copy-start(bf16[1,320,512]{2,1,0:T(8,128)(2,1)} %param.16) | copy-start | bytes 983044
  7.2 44.0 %all-reduce.18.cloned.1.call-start = ((), (), s32[]{:S(2)}) async-start(), calls=%async_computation.6 | async-start | bytes 327680 | tf_op jit(solution)/shard_map/psum | solution.py:132
  19.2 79.8 %reduce-scatter.6.cloned.1.call-start = ((), (), s32[]{:S(2)}) async-start(), calls=%async_computation.5 | async-start | bytes 5242880 | tf_op jit(solution)/shard_map/reduce_scatter | solution.py:131
  26.1 25.9 %copy-start.19 = (f32[1,16]{1,0:T(1,128)S(1)}, f32[1,16]{1,0:T(1,128)}, u32[]{:S(2)}) copy-start(f32[1,16]{1,0:T(1,128)} %param.20) | copy-start | bytes 196
  26.1 107.5 %reduce-scatter.8.cloned.1.call-start = ((), (), s32[]{:S(2)}) async-start(), calls=%async_computation.7 | async-start | bytes 2621440 | tf_op jit(solution)/shard_map/reduce_scatter | solution.py:174
  31.9 69.9 %copy-start.27 = (f32[1,16]{1,0:T(1,128)S(1)}, f32[1,16]{1,0:T(1,128)}, u32[]{:S(2)}) copy-start(f32[1,16]{1,0:T(1,128)} %param.22) | copy-start | bytes 196
  31.9 161.1 %reduce-scatter.4.cloned.1.call-start = ((), (), s32[]{:S(2)}) async-start(), calls=%async_computation.3 | async-start | bytes 5242880 | tf_op jit(solution)/shard_map/reduce_scatter | solution.py:131
  32.1 21.2 %copy-start.21 = (f32[16]{0:T(128)}, f32[16]{0:T(128)S(1)}, u32[]{:S(2)}) copy-start(f32[16]{0:T(128)S(1)} %negate_bitcast_fusion) | copy-start | bytes 196
  32.2 68.4 %copy-start.13 = (f32[1,1,256]{2,1,0:T(1,128)}, f32[1,1,256]{2,1,0:T(1,128)S(1)}, u32[]{:S(2)}) copy-start(f32[1,1,256]{2,1,0:T(1,128)S(1)} %get-tuple-element.44) | copy-start | bytes 3076
  32.2 72.6 %copy-start.15 = (f32[1,1,256]{2,1,0:T(1,128)}, f32[1,1,256]{2,1,0:T(1,128)S(1)}, u32[]{:S(2)}) copy-start(f32[1,1,256]{2,1,0:T(1,128)S(1)} %get-tuple-element.46) | copy-start | bytes 3076
  52.0 97.6 %copy-start.17 = (f32[16,128]{1,0:T(8,128)}, f32[16,128]{1,0:T(8,128)S(1)}, u32[]{:S(2)}) copy-start(f32[16,128]{1,0:T(8,128)S(1)} %get-tuple-element.37) | copy-start | bytes 24580
  52.4 97.3 %copy-start.18 = (f32[16,128]{1,0:T(8,128)}, f32[16,128]{1,0:T(8,128)S(1)}, u32[]{:S(2)}) copy-start(f32[16,128]{1,0:T(8,128)S(1)} %copy.57) | copy-start | bytes 24580
  55.4 94.3 %copy-start.10 = (f32[128,128]{1,0:T(8,128)}, f32[128,128]{1,0:T(8,128)S(1)}, u32[]{:S(2)}) copy-start(f32[128,128]{1,0:T(8,128)S(1)} %fusion.125) | copy-start | bytes 196612
  100.6 33.0 %copy-start.11 = (f32[1,1024]{1,0:T(1,128)S(1)}, f32[1,1024]{1,0:T(1,128)}, u32[]{:S(2)}) copy-start(f32[1,1024]{1,0:T(1,128)} %param.23) | copy-start | bytes 12292
  101.8 45.4 %copy-start.8 = (f32[1,128,1024]{1,2,0:T(8,128)}, f32[1,128,1024]{1,2,0:T(8,128)S(1)}, u32[]{:S(2)}) copy-start(f32[1,128,1024]{1,2,0:T(8,128)S(1)} %get-tuple-element.24) | copy-start | bytes 1572868
  147.3 80.4 %all-reduce.20.cloned.1.call-start = ((), (), s32[]{:S(2)}) async-start(), calls=%async_computation.10 | async-start | bytes 655360 | tf_op jit(solution)/shard_map/psum | solution.py:132
  161.7 90.6 %all-gather.6.cloned.1.call-start = ((), (), s32[]{:S(2)}) async-start(), calls=%async_computation.8 | async-start | bytes 2621440 | tf_op jit(solution)/shard_map/all_gather | solution.py:206
  194.6 35.5 %copy-start.9 = (f32[1,128,256]{1,2,0:T(8,128)S(1)}, f32[1,128,256]{1,2,0:T(8,128)}, u32[]{:S(2)}) copy-start(f32[1,128,256]{1,2,0:T(8,128)} %get-tuple-element.23) | copy-start | bytes 393220
  194.6 36.5 %copy-start.14 = (f32[1,1,256]{2,1,0:T(1,128)S(1)}, f32[1,1,256]{2,1,0:T(1,128)}, u32[]{:S(2)}) copy-start(f32[1,1,256]{2,1,0:T(1,128)} %copy-done.13) | copy-start | bytes 3076
  194.6 36.5 %copy-start.16 = (f32[1,1,256]{2,1,0:T(1,128)S(1)}, f32[1,1,256]{2,1,0:T(1,128)}, u32[]{:S(2)}) copy-start(f32[1,1,256]{2,1,0:T(1,128)} %copy-done.15) | copy-start | bytes 3076
  196.5 36.1 %copy-start.20 = (f32[1,16]{1,0:T(1,128)S(1)}, f32[1,16]{1,0:T(1,128)}, u32[]{:S(2)}) copy-start(f32[1,16]{1,0:T(1,128)} %param.20) | copy-start | bytes 196
  196.5 36.1 %copy-start.22 = (f32[16]{0:T(128)S(1)}, f32[16]{0:T(128)}, u32[]{:S(2)}) copy-start(f32[16]{0:T(128)} %copy-done.21) | copy-start | bytes 196
  196.5 36.7 %copy-start.28 = (f32[1,16]{1,0:T(1,128)S(1)}, f32[1,16]{1,0:T(1,128)}, u32[]{:S(2)}) copy-start(f32[1,16]{1,0:T(1,128)} %param.22) | copy-start | bytes 196
  197.9 73.4 %all-gather.8.cloned.1.call-start = ((), (), s32[]{:S(2)}) async-start(), calls=%async_computation.9 | async-start | bytes 1310720 | tf_op jit(solution)/shard_map/all_gather | solution.py:173
  198.6 91.0 %all-gather.4.cloned.1.call-start = ((), (), s32[]{:S(2)}) async-start(), calls=%async_computation.4 | async-start | bytes 1310720 | tf_op jit(solution)/shard_map/all_gather | solution.py:164
  236.7 22.5 %copy-start.2 = (bf16[1,128,512]{2,1,0:T(8,128)(2,1)S(1)}, bf16[1,128,512]{2,1,0:T(8,128)(2,1)}, u32[]{:S(2)}) copy-start(bf16[1,128,512]{2,1,0:T(8,128)(2,1)} %param.13) | copy-start | bytes 393220
  267.9 9.3 %copy-start.6 = (bf16[1,128,512]{2,1,0:T(8,128)(2,1)S(1)}, bf16[1,128,512]{2,1,0:T(8,128)(2,1)}, u32[]{:S(2)}) copy-start(bf16[1,128,512]{2,1,0:T(8,128)(2,1)} %param.14) | copy-start | bytes 393220
  267.9 9.3 %copy-start.25 = (f32[128]{0:T(128)S(1)}, f32[128]{0:T(128)}, u32[]{:S(2)}) copy-start(f32[128]{0:T(128)} %get-tuple-element.48) | copy-start | bytes 1540
  267.9 21.8 %copy-start.4 = (bf16[1,128,512]{2,1,0:T(8,128)(2,1)S(1)}, bf16[1,128,512]{2,1,0:T(8,128)(2,1)}, u32[]{:S(2)}) copy-start(bf16[1,128,512]{2,1,0:T(8,128)(2,1)} %param.12) | copy-start | bytes 393220
  277.2 17.2 %copy-start.1 = (bf16[128,8192]{0,1:T(8,128)(2,1)S(1)}, bf16[128,8192]{0,1:T(8,128)(2,1)}, u32[]{:S(2)}) copy-start(bf16[128,8192]{0,1:T(8,128)(2,1)} %all-gather.6.cloned.1.call-done) | copy-start | bytes 6291460
  277.4 25.7 %collective-permute-start.1 = (bf16[128,512]{1,0:T(8,128)(2,1)S(1)}, bf16[128,512]{1,0:T(8,128)(2,1)S(1)}, u32[]{:S(2)}, u32[]{:S(2)}) collective-permute-start(bf16[128,512]{1,0:T(8,128)(2,1)S(1)} %fusion.91), channel_id=1, source_target_pairs={{0,28},{4,0},{8,4},{12,8},{16,12},{20,16},{24,20},{28,24},{1,29},{... | collective-permute-start | bytes 393224 | tf_op jit(solution)/shard_map/ppermute | solution.py:16
  292.9 10.1 %collective-permute-start = (bf16[128,512]{1,0:T(8,128)(2,1)S(1)}, bf16[128,512]{1,0:T(8,128)(2,1)S(1)}, u32[]{:S(2)}, u32[]{:S(2)}) collective-permute-start(bf16[128,512]{1,0:T(8,128)(2,1)S(1)} %fusion.17), channel_id=1, source_target_pairs={{0,4},{4,8},{8,12},{12,16},{16,20},{20,24},{24,28},{28,0},{1,5},{5... | collective-permute-start | bytes 393224 | tf_op jit(solution)/shard_map/ppermute | solution.py:16
  (7 other events, 41.0 us)
Sparse Core Ops, SparseCore 0:
  19.3 31.8 all-reduce.17
  54.4 44.5 reduce-scatter.5
  102.1 31.4 reduce-scatter.7
  147.4 45.5 reduce-scatter.3
  195.2 32.4 all-reduce.19
  229.7 22.5 all-gather.5
  254.4 16.8 all-gather.7
  272.9 16.7 all-gather.3
where the time goes:
time: 312 us; the launch traced here: 311 us
  waiting for transfers between devices  178 us (57%)
  matrix products  61.8 us (20%)
  blocking collectives  20.4 us (7%)
  other arithmetic  17.4 us (6%)
  between operations  14.7 us (5%)
  local copies, waits for them, and re-layouts  12.5 us (4%)
  starting transfers between devices  6.58 us (2%)
    reduce_scatter x2, waiting for transfers between devices, project(): own_xz = lax.psum_scatter(part_xz, 'dp', scatter_dimension=1, tiled=True)  74.9 us
    psum x2, waiting for transfers between devices, project(): whole_cols = lax.psum(part_bcdt, 'dp')  47.7 us
    reduce_scatter x1, waiting for transfers between devices, per_device(): lax.psum_scatter(times_transposed(cot_rows, local_out), 'dp', scatter_dim...  27.5 us
    dot_general x3, matrix products, transposed_times(): lax.dot_general(left, right, (((0,), (0,)), ((), ())), preferred_element_...  15.6 us
    all_gather x1, waiting for transfers between devices, per_device(): round_xz = lax.all_gather(own_round, 'dp', axis=1, tiled=True)  15.6 us
    dot_general x4, matrix products, times_transposed(): lax.dot_general(left, right, (((1,), (1,)), ((), ())), preferred_element_...  15.5 us
    psum x2, blocking collectives, feature_sum(): return lax.psum(jnp.sum(values, axis=1), 'dp')  14.1 us
    dot_general x2, matrix products, project(): part_xz = jnp.dot(normed, local_xz, preferred_element_type=jnp.float32)  13.5 us
  transfers between devices with their start and end apart: 10, of which 8 were waited for; matrix products, arithmetic and copies ran while one was open for 25% of the time, Pallas kernels for 0%

commit v1 on v0

--- a/solution.py
+++ b/solution.py
@@ -129,7 +129,11 @@
         part_xz = jnp.dot(normed, local_xz, preferred_element_type=jnp.float32)
         part_bcdt = times_transposed(normed, local_bcdt)
         own_xz = lax.psum_scatter(part_xz, "dp", scatter_dimension=1, tiled=True)
-        whole_cols = lax.psum(part_bcdt, "dp")
+        whole_cols = part_bcdt
+        for hop in (1, 2):
+            whole_cols = whole_cols + lax.ppermute(
+                whole_cols, "dp", [(dev, dev ^ hop) for dev in range(4)]
+            )
         pre_part = whole_cols[:, :map_cols]
         maps = whole_act(pre_part).astype(jnp.bfloat16)
         own_dt = lax.dynamic_slice_in_dim(whole_cols[:, map_cols:], head_first, own_heads, 1)

time: 312 us -> 281 us (0.901)
  waiting for transfers between devices: 178 us -> 145 us
  other arithmetic: 17.4 us -> 21.5 us
    reduce_scatter x2, waiting for transfers between devices: 74.9 us -> 52.7 us  [project(): own_xz = lax.psum_scatter(part_xz, 'dp', scatter_dimension=1, tiled=True)]
    psum x2 -> x1, waiting for transfers between devices: 47.7 us -> 26.1 us  [per_device(): summed = lax.psum(map_part, 'dp')]
    ppermute x0 -> x4, waiting for transfers between devices: none -> 9.65 us  [project(): lax.ppermute(whole_cols, 'dp', [(dev, dev ^ hop) for dev in range(4)])]
  transfers between devices with their start and end apart: 10 -> 13, of which waited for: 8 -> 10; matrix products, arithmetic and copies ran while one was open for 25% -> 26% of each run, Pallas kernels for 0% -> 0%
where the time goes in v1:
time: 281 us
  waiting for transfers between devices  145 us (52%)
  matrix products  59.7 us (21%)
  other arithmetic  21.5 us (8%)
  blocking collectives  20.6 us (7%)
  between operations  14.8 us (5%)
  local copies, waits for them, and re-layouts  9.77 us (3%)
  starting transfers between devices  8.99 us (3%)
    reduce_scatter x2, waiting for transfers between devices, project(): own_xz = lax.psum_scatter(part_xz, 'dp', scatter_dimension=1, tiled=True)  52.7 us
    reduce_scatter x1, waiting for transfers between devices, per_device(): lax.psum_scatter(times_transposed(cot_rows, local_out), 'dp', scatter_dim...  26.3 us
    psum x1, waiting for transfers between devices, per_device(): summed = lax.psum(map_part, 'dp')  26.1 us
    all_gather x1, waiting for transfers between devices, per_device(): round_xz = lax.all_gather(own_round, 'dp', axis=1, tiled=True)  18.6 us
    dot_general x3, matrix products, transposed_times(): lax.dot_general(left, right, (((0,), (0,)), ((), ())), preferred_element_...  15.6 us
    psum x2, blocking collectives, feature_sum(): return lax.psum(jnp.sum(values, axis=1), 'dp')  14.3 us
    dot_general x2, matrix products, project(): part_xz = jnp.dot(normed, local_xz, preferred_element_type=jnp.float32)  13.5 us
    dot_general x4, matrix products, times_transposed(): lax.dot_general(left, right, (((1,), (1,)), ((), ())), preferred_element_...  13.2 us
  transfers between devices with their start and end apart: 13, of which 10 were waited for; matrix products, arithmetic and copies ran while one was open for 26% of the time, Pallas kernels for 0%

profile of v1, /device:TPU:0, one launch (start us, length us, event | category | flops | bytes accessed | tf_op | source)
XLA Modules:
  0.0 280.5 jit_solution(5150698043640572512)
XLA Ops:
  8.3 8.4 %psum.51 = f32[128]{0:T(128)S(1)} all-reduce(f32[128]{0:T(128)S(1)} %fusion.86), channel_id=1, replica_groups=mesh['section'=8,'dp'=4] {'dp'}, use_global_device_ids=true, to_apply=%region_7.8 | all-reduce | flops 128 | bytes 1024 | tf_op jit(solution)/shard_map/psum | solution.py:79
  17.2 6.8 %fusion.2 = f32[128,8192]{1,0:T(8,128)} fusion(bf16[1,512,8192]{2,1,0:T(8,128)(2,1)} %param.15, bf16[1,128,512]{2,1,0:T(8,128)(2,1)} %param.13, f32[128]{0:T(128)S(1)} %get-tuple-element.48), kind=kOutput, calls=%fused_computation.3 | convolution fusion | flops 1073938432 | bytes 12714496 | tf_op jit(solution)/shard_map/dot_general | solution.py:129
  24.9 5.0 %fusion.6 = f32[128,4096]{1,0:T(8,128)} fusion(bf16[1,4096,512]{2,1,0:T(8,128)(2,1)} %param.17, bf16[1,128,512]{2,1,0:T(8,128)(2,1)S(1)} %copy-done.5), kind=kOutput, calls=%fused_computation.8 | convolution fusion | flops 536870912 | bytes 6422528 | tf_op jit(solution)/shard_map/dot_general | solution.py:67
  33.2 5.0 %collective-permute-done.4 = f32[128,320]{0,1:T(8,128)S(1)} collective-permute-done((f32[128,320]{0,1:T(8,128)S(1)}, f32[128,320]{0,1:T(8,128)S(1)}, u32[]{:S(2)}, u32[]{:S(2)}) %collective-permute-start.4) | collective-permute-done | bytes 163872 | tf_op jit(solution)/shard_map/ppermute | solution.py:134
  41.0 28.0 %reduce-scatter.6.cloned.1.call-done = f32[128,2048]{1,0:T(8,128)} async-done(((f32[128,8192]{1,0:T(8,128)}), f32[128,2048]{1,0:T(8,128)}) %reduce-scatter.6.cloned.1.call-update) | async-done | bytes 1048592 | tf_op jit(solution)/shard_map/reduce_scatter | solution.py:131
  69.0 1.5 copy.55
  71.9 4.3 %multiply_reduce_fusion.3 = (f32[128]{0:T(128)}, f32[1,128,16,64]{1,3,2,0:T(8,128)}, f32[1,128,16,64]{1,3,2,0:T(8,128)}) fusion(f32[1,128,16,2,64]{1,4,3,2,0:T(8,128)S(1)} %bitcast.271, f32[1,128,16,64]{1,3,2,0:T(8,128)S(1)} %bitcast.283, f32[16]{0:T(128)} %bitcast.317, f32[128,16,64]{0,2,1:T(8,128)S(1)} %bitcast.284, f32[16,128]{1,0:T(8,128)S(1)} %copy-done.30, ...), kind=kOutput, calls=%fused_computation.80 | convolution fusion | flops 203816832 | bytes 2728960 | tf_op jit(solution)/shard_map/jvp(bhts,bshp->bthp)/dot_general | solution.py:60
  77.5 26.3 %reduce-scatter.8.cloned.1.call-done = f32[128,1024]{1,0:T(8,128)} async-done(((f32[128,4096]{1,0:T(8,128)}), f32[128,1024]{1,0:T(8,128)}) %reduce-scatter.8.cloned.1.call-update) | async-done | bytes 524304 | tf_op jit(solution)/shard_map/reduce_scatter | solution.py:178
  104.9 5.9 %all-reduce.13 = (f32[128]{0:T(128)S(1)}, f32[128]{0:T(128)S(1)}, f32[128]{0:T(128)S(1)}) all-reduce(f32[128]{0:T(128)} %fusion.84, f32[128]{0:T(128)S(1)} %multiply_reduce_fusion.2, f32[128]{0:T(128)} %get-tuple-element.18), channel_id=1, replica_groups=mesh['section'=8,'dp'=4] {'dp'}, use_global_device_ids=true, to_apply=%region_1.0 | all-reduce | flops 384 | bytes 3072 | tf_op jit(solution)/shard_map/psum | solution.py:79
  110.8 6.7 %fusion.4 = f32[128,8192]{1,0:T(8,128)} fusion(bf16[1,512,8192]{2,1,0:T(8,128)(2,1)} %param.15, bf16[1,128,512]{2,1,0:T(8,128)(2,1)S(1)} %copy-done.3, f32[128]{0:T(128)S(1)} %add_rsqrt_fusion.3), kind=kOutput, calls=%fused_computation.5 | convolution fusion | flops 1073938432 | bytes 12714496 | tf_op jit(solution)/shard_map/dot_general | solution.py:129
  117.8 2.0 multiply_convert_fusion
  121.1 2.0 fusion.95
  123.1 2.4 fusion.10
  126.5 3.0 %fusion.32 = (f32[16,128]{1,0:T(8,128)S(1)}, f32[16,128]{1,0:T(8,128)S(1)}, f32[16,128]{1,0:T(8,128)}, f32[128,128]{1,0:T(8,128)S(1)}) fusion(f32[16,128]{1,0:T(8,128)S(1)} %copy-done.31, f32[128,128]{1,0:T(8,128)S(1)} %copy-done.12, f32[16,128]{1,0:T(8,128)S(1)} %copy-done.32, pred[128,128]{1,0:T(8,128)(4,1)S(1)} %copy-done.22, ...), kind=kOutput, calls=%fused_computation.47 | convolution fusion | flops 205891584 | bytes 1769472 | tf_op jit(solution)/shard_map/transpose(jvp(bhts,bshp->bthp))/dot_general | solution.py:60
  129.7 1.7 collective-permute-start.1
  133.0 3.4 %collective-permute-done.1 = f32[128,320]{0,1:T(8,128)S(1)} collective-permute-done((f32[128,320]{0,1:T(8,128)S(1)}, f32[128,320]{0,1:T(8,128)S(1)}, u32[]{:S(2)}, u32[]{:S(2)}) %collective-permute-start.1) | collective-permute-done | bytes 163872 | tf_op jit(solution)/shard_map/ppermute | solution.py:134
  136.4 1.5 multiply_bitcast_fusion.1
  138.7 24.7 %reduce-scatter.4.cloned.1.call-done = f32[128,2048]{1,0:T(8,128)} async-done(((f32[128,8192]{1,0:T(8,128)}), f32[128,2048]{1,0:T(8,128)}) %reduce-scatter.4.cloned.1.call-update) | async-done | bytes 1048592 | tf_op jit(solution)/shard_map/reduce_scatter | solution.py:131
  163.4 1.5 copy.49
  165.0 2.6 broadcast_multiply_fusion.1
  171.1 26.1 %all-reduce.16.cloned.1.call-done = f32[128,320]{0,1:T(8,128)} async-done(((f32[128,320]{0,1:T(8,128)}), f32[128,320]{0,1:T(8,128)}) %all-reduce.16.cloned.1.call-update) | async-done | bytes 163856 | tf_op jit(solution)/shard_map/psum | solution.py:195
  199.7 3.3 %multiply_reduce_fusion.4 = (f32[128]{0:T(128)S(1)}, f32[1,128,16,64]{1,3,2,0:T(8,128)S(1)}) fusion(f32[1,128,16,2,64]{1,4,3,2,0:T(8,128)S(1)} %bitcast.276, f32[1,128,16,64]{1,3,2,0:T(8,128)} %bitcast.288, f32[16]{0:T(128)S(1)} %bitcast.319, f32[128,16,64]{0,2,1:T(8,128)} %bitcast.289, f32[16,128]{1,0:T(8,128)} %get-tuple-element.33, ...), kind=kOutput, calls=%fused_computation.94 | convolution fusion | flops 203816832 | bytes 2204672 | tf_op jit(solution)/shard_map/jvp(bhts,bshp->bthp)/dot_general | solution.py:60
  203.3 18.6 %all-gather.6.cloned.1.call-done = bf16[128,8192]{0,1:T(8,128)(2,1)} async-done(((bf16[128,2048]{0,1:T(8,128)(2,1)}), bf16[128,8192]{0,1:T(8,128)(2,1)}) %all-gather.6.cloned.1.call-update) | async-done | bytes 2097168 | tf_op jit(solution)/shard_map/all_gather | solution.py:210
  221.8 6.9 %fusion = f32[128,512]{1,0:T(8,128)S(1)} fusion(bf16[128,8192]{0,1:T(8,128)(2,1)} %all-gather.6.cloned.1.call-done, bf16[1,512,8192]{2,1,0:T(8,128)(2,1)} %param.15), kind=kOutput, calls=%fused_computation.1 | convolution fusion | flops 1073741824 | bytes 10747904 | tf_op jit(solution)/shard_map/dot_general | solution.py:67
  229.1 6.3 %all-reduce.12 = (f32[128]{0:T(128)S(1)}, f32[128]{0:T(128)S(1)}) all-reduce(f32[128]{0:T(128)S(1)} %get-tuple-element.52, f32[128]{0:T(128)S(1)} %get-tuple-element.54), channel_id=1, replica_groups=mesh['section'=8,'dp'=4] {'dp'}, use_global_device_ids=true, to_apply=%region_5.6 | all-reduce | flops 256 | bytes 2048 | tf_op jit(solution)/shard_map/psum | solution.py:83
  237.4 3.3 %all-gather.8.cloned.1.call-done = bf16[128,4096]{1,0:T(8,128)(2,1)} async-done(((bf16[128,1024]{1,0:T(8,128)(2,1)}), bf16[128,4096]{1,0:T(8,128)(2,1)}) %all-gather.8.cloned.1.call-update) | async-done | bytes 1048592 | tf_op jit(solution)/shard_map/all_gather | solution.py:177
  240.7 5.9 %convolution_bitcast_fusion.1 = f32[1,4096,512]{2,1,0:T(8,128)} fusion(bf16[128,4096]{1,0:T(8,128)(2,1)} %all-gather.8.cloned.1.call-done, bf16[1,128,512]{2,1,0:T(8,128)(2,1)S(1)} %copy-done.5), kind=kOutput, calls=%fused_computation.7 | convolution fusion | flops 536870912 | bytes 9568256 | tf_op jit(solution)/shard_map/dot_general | solution.py:73
  246.7 4.3 %collective-permute-start.5 = (bf16[128,512]{1,0:T(8,128)(2,1)S(1)}, bf16[128,512]{1,0:T(8,128)(2,1)S(1)}, u32[]{:S(2)}, u32[]{:S(2)}) collective-permute-start(bf16[128,512]{1,0:T(8,128)(2,1)S(1)} %fusion.91), channel_id=1, source_target_pairs={{0,28},{4,0},{8,4},{12,8},{16,12},{20,16},{24,20},{28,24},{1,29},{... | collective-permute-start | bytes 393224 | tf_op jit(solution)/shard_map/ppermute | solution.py:16
  251.0 8.0 %all-gather.4.cloned.1.call-done = bf16[128,4096]{1,0:T(8,128)(2,1)} async-done(((bf16[128,1024]{1,0:T(8,128)(2,1)}), bf16[128,4096]{1,0:T(8,128)(2,1)}) %all-gather.4.cloned.1.call-update) | async-done | bytes 1048592 | tf_op jit(solution)/shard_map/all_gather | solution.py:168
  259.0 3.2 %fusion.17 = bf16[128,512]{1,0:T(8,128)(2,1)S(1)} fusion(bf16[128,4096]{1,0:T(8,128)(2,1)} %all-gather.4.cloned.1.call-done, bf16[1,4096,512]{2,1,0:T(8,128)(2,1)} %param.17, bf16[1,128,512]{2,1,0:T(8,128)(2,1)S(1)} %copy-done.3), kind=kOutput, calls=%fused_computation.28 | convolution fusion | flops 537067520 | bytes 5505024 | tf_op jit(solution)/shard_map/dot_general | solution.py:167
  262.2 1.5 collective-permute-start.2
  263.8 8.6 %convolution_bitcast_fusion = f32[1,512,8192]{2,1,0:T(8,128)} fusion(bf16[128,8192]{0,1:T(8,128)(2,1)S(1)} %copy-done.1, bf16[1,128,512]{2,1,0:T(8,128)(2,1)S(1)} %copy-done.2, f32[128]{0:T(128)S(1)} %copy-done.17), kind=kOutput, calls=%fused_computation | convolution fusion | flops 1073938432 | bytes 19005952 | tf_op jit(solution)/shard_map/dot_general | solution.py:73
  (161 shorter events, 27.1 us)
Async XLA Ops:
  7.2 61.8 %reduce-scatter.6.cloned.1.call-start = ((), (), s32[]{:S(2)}) async-start(), calls=%async_computation.5 | async-start | bytes 5242880 | tf_op jit(solution)/shard_map/reduce_scatter | solution.py:131
  24.1 79.6 %reduce-scatter.8.cloned.1.call-start = ((), (), s32[]{:S(2)}) async-start(), calls=%async_computation.6 | async-start | bytes 2621440 | tf_op jit(solution)/shard_map/reduce_scatter | solution.py:178
  29.9 133.4 %reduce-scatter.4.cloned.1.call-start = ((), (), s32[]{:S(2)}) async-start(), calls=%async_computation.3 | async-start | bytes 5242880 | tf_op jit(solution)/shard_map/reduce_scatter | solution.py:131
  30.3 1.5 collective-permute-start.3
  30.4 40.1 %copy-start.18 = (f32[1,1,256]{2,1,0:T(1,128)}, f32[1,1,256]{2,1,0:T(1,128)S(1)}, u32[]{:S(2)}) copy-start(f32[1,1,256]{2,1,0:T(1,128)S(1)} %get-tuple-element.43) | copy-start | bytes 3076
  30.5 40.2 %copy-start.26 = (f32[1,1,256]{2,1,0:T(1,128)}, f32[1,1,256]{2,1,0:T(1,128)S(1)}, u32[]{:S(2)}) copy-start(f32[1,1,256]{2,1,0:T(1,128)S(1)} %get-tuple-element.42) | copy-start | bytes 3076
  30.5 40.2 %copy-start.28 = (f32[1,1,256]{2,1,0:T(1,128)}, f32[1,1,256]{2,1,0:T(1,128)S(1)}, u32[]{:S(2)}) copy-start(f32[1,1,256]{2,1,0:T(1,128)S(1)} %get-tuple-element.44) | copy-start | bytes 3076
  30.5 45.7 %copy-start.24 = (f32[1,1,256]{2,1,0:T(1,128)}, f32[1,1,256]{2,1,0:T(1,128)S(1)}, u32[]{:S(2)}) copy-start(f32[1,1,256]{2,1,0:T(1,128)S(1)} %get-tuple-element.41) | copy-start | bytes 3076
  30.5 45.7 %copy-start.14 = (f32[1,1,1024]{2,1,0:T(1,128)}, f32[1,1,1024]{2,1,0:T(1,128)S(1)}, u32[]{:S(2)}) copy-start(f32[1,1,1024]{2,1,0:T(1,128)S(1)} %get-tuple-element.39) | copy-start | bytes 12292
  30.5 40.1 %copy-start.33 = (f32[16]{0:T(128)}, f32[16]{0:T(128)S(1)}, u32[]{:S(2)}) copy-start(f32[16]{0:T(128)S(1)} %negate_bitcast_fusion) | copy-start | bytes 196
  31.8 6.3 %collective-permute-start.4 = (f32[128,320]{0,1:T(8,128)S(1)}, f32[128,320]{0,1:T(8,128)S(1)}, u32[]{:S(2)}, u32[]{:S(2)}) collective-permute-start(f32[128,320]{0,1:T(8,128)S(1)} %add.241), channel_id=1, source_target_pairs={{0,2},{1,3},{2,0},{3,1},{4,6},{5,7},{6,4},{7,5},{8,10},{9,11},{10,... | collective-permute-start | bytes 491528 | tf_op jit(solution)/shard_map/ppermute | solution.py:134
  32.5 43.7 %copy-start.21 = (pred[128,128]{1,0:T(8,128)(4,1)}, pred[128,128]{1,0:T(8,128)(4,1)S(1)}, u32[]{:S(2)}) copy-start(pred[128,128]{1,0:T(8,128)(4,1)S(1)} %iota_compare_fusion) | copy-start | bytes 49156
  39.0 32.9 %copy-start.30 = (f32[16,128]{1,0:T(8,128)S(1)}, f32[16,128]{1,0:T(8,128)}, u32[]{:S(2)}) copy-start(f32[16,128]{1,0:T(8,128)} %get-tuple-element.35) | copy-start | bytes 24580
  40.8 35.4 %copy-start.6 = (bf16[1,128,256]{1,2,0:T(8,128)(2,1)}, bf16[1,128,256]{1,2,0:T(8,128)(2,1)S(1)}, u32[]{:S(2)}) copy-start(bf16[1,128,256]{1,2,0:T(8,128)(2,1)S(1)} %get-tuple-element.20) | copy-start | bytes 196612
  41.0 35.2 %copy-start.11 = (f32[128,128]{1,0:T(8,128)}, f32[128,128]{1,0:T(8,128)S(1)}, u32[]{:S(2)}) copy-start(f32[128,128]{1,0:T(8,128)S(1)} %fusion.125) | copy-start | bytes 196612
  70.6 33.2 %copy-start.13 = (f32[1,1024]{1,0:T(1,128)S(1)}, f32[1,1024]{1,0:T(1,128)}, u32[]{:S(2)}) copy-start(f32[1,1024]{1,0:T(1,128)} %param.23) | copy-start | bytes 12292
  71.9 45.7 %copy-start.8 = (f32[1,128,1024]{1,2,0:T(8,128)}, f32[1,128,1024]{1,2,0:T(8,128)S(1)}, u32[]{:S(2)}) copy-start(f32[1,128,1024]{1,2,0:T(8,128)S(1)} %get-tuple-element.22) | copy-start | bytes 1572868
  117.6 79.6 %all-reduce.16.cloned.1.call-start = ((), (), s32[]{:S(2)}) async-start(), calls=%async_computation.8 | async-start | bytes 327680 | tf_op jit(solution)/shard_map/psum | solution.py:195
  121.0 8.7 %collective-permute-start = (f32[128,320]{0,1:T(8,128)S(1)}, f32[128,320]{0,1:T(8,128)S(1)}, u32[]{:S(2)}, u32[]{:S(2)}) collective-permute-start(f32[128,320]{0,1:T(8,128)S(1)} %fusion.82), channel_id=1, source_target_pairs={{0,1},{1,0},{2,3},{3,2},{4,5},{5,4},{6,7},{7,6},{8,9},{9,8},{10,11... | collective-permute-start | bytes 491528 | tf_op jit(solution)/shard_map/ppermute | solution.py:134
  129.5 35.5 %copy-start.4 = (f32[1,128,1024]{1,2,0:T(8,128)S(1)}, f32[1,128,1024]{1,2,0:T(8,128)}, u32[]{:S(2)}) copy-start(f32[1,128,1024]{1,2,0:T(8,128)} %get-tuple-element.17) | copy-start | bytes 1572868
  129.7 6.7 %collective-permute-start.1 = (f32[128,320]{0,1:T(8,128)S(1)}, f32[128,320]{0,1:T(8,128)S(1)}, u32[]{:S(2)}, u32[]{:S(2)}) collective-permute-start(f32[128,320]{0,1:T(8,128)S(1)} %add.221), channel_id=1, source_target_pairs={{0,2},{1,3},{2,0},{3,1},{4,6},{5,7},{6,4},{7,5},{8,10},{9,11},{10,... | collective-permute-start | bytes 491528 | tf_op jit(solution)/shard_map/ppermute | solution.py:134
  138.6 83.2 %all-gather.6.cloned.1.call-start = ((), (), s32[]{:S(2)}) async-start(), calls=%async_computation.7 | async-start | bytes 2621440 | tf_op jit(solution)/shard_map/all_gather | solution.py:210
  165.0 32.2 %copy-start.19 = (f32[1,1,256]{2,1,0:T(1,128)S(1)}, f32[1,1,256]{2,1,0:T(1,128)}, u32[]{:S(2)}) copy-start(f32[1,1,256]{2,1,0:T(1,128)} %copy-done.18) | copy-start | bytes 3076
  165.0 33.2 %copy-start.25 = (f32[1,1,256]{2,1,0:T(1,128)S(1)}, f32[1,1,256]{2,1,0:T(1,128)}, u32[]{:S(2)}) copy-start(f32[1,1,256]{2,1,0:T(1,128)} %copy-done.24) | copy-start | bytes 3076
  167.6 30.7 %copy-start.29 = (f32[1,1,256]{2,1,0:T(1,128)S(1)}, f32[1,1,256]{2,1,0:T(1,128)}, u32[]{:S(2)}) copy-start(f32[1,1,256]{2,1,0:T(1,128)} %copy-done.28) | copy-start | bytes 3076
  167.6 32.1 %copy-start.23 = (pred[128,128]{1,0:T(8,128)(4,1)S(1)}, pred[128,128]{1,0:T(8,128)(4,1)}, u32[]{:S(2)}) copy-start(pred[128,128]{1,0:T(8,128)(4,1)} %copy-done.21) | copy-start | bytes 49156
  167.6 32.1 %copy-start.39 = (f32[1,16]{1,0:T(1,128)S(1)}, f32[1,16]{1,0:T(1,128)}, u32[]{:S(2)}) copy-start(f32[1,16]{1,0:T(1,128)} %param.22) | copy-start | bytes 196
  169.9 70.7 %all-gather.8.cloned.1.call-start = ((), (), s32[]{:S(2)}) async-start(), calls=%async_computation.9 | async-start | bytes 1310720 | tf_op jit(solution)/shard_map/all_gather | solution.py:177
  170.5 88.5 %all-gather.4.cloned.1.call-start = ((), (), s32[]{:S(2)}) async-start(), calls=%async_computation.4 | async-start | bytes 1310720 | tf_op jit(solution)/shard_map/all_gather | solution.py:168
  203.3 33.0 %copy-start.17 = (f32[128]{0:T(128)S(1)}, f32[128]{0:T(128)}, u32[]{:S(2)}) copy-start(f32[128]{0:T(128)} %copy-done.16) | copy-start | bytes 1540
  246.7 25.6 %collective-permute-start.5 = (bf16[128,512]{1,0:T(8,128)(2,1)S(1)}, bf16[128,512]{1,0:T(8,128)(2,1)S(1)}, u32[]{:S(2)}, u32[]{:S(2)}) collective-permute-start(bf16[128,512]{1,0:T(8,128)(2,1)S(1)} %fusion.91), channel_id=1, source_target_pairs={{0,28},{4,0},{8,4},{12,8},{16,12},{20,16},{24,20},{28,24},{1,29},{... | collective-permute-start | bytes 393224 | tf_op jit(solution)/shard_map/ppermute | solution.py:16
  262.2 10.1 %collective-permute-start.2 = (bf16[128,512]{1,0:T(8,128)(2,1)S(1)}, bf16[128,512]{1,0:T(8,128)(2,1)S(1)}, u32[]{:S(2)}, u32[]{:S(2)}) collective-permute-start(bf16[128,512]{1,0:T(8,128)(2,1)S(1)} %fusion.17), channel_id=1, source_target_pairs={{0,4},{4,8},{8,12},{12,16},{16,20},{20,24},{24,28},{28,0},{1,5},{5... | collective-permute-start | bytes 393224 | tf_op jit(solution)/shard_map/ppermute | solution.py:16
  (21 other events, 203.3 us)
Sparse Core Ops, SparseCore 0:
  24.2 44.8 reduce-scatter.5
  72.3 31.4 reduce-scatter.7
  117.7 45.6 reduce-scatter.3
  165.6 31.5 all-reduce.15
  199.2 22.5 all-gather.5
  223.8 16.8 all-gather.7
  242.2 16.7 all-gather.3
